TPU v7x, 256 devices: a whole 4x4x8 slice. The times are simulated.
256 devices in a mesh: group: 32 (over x, z), span: 8 (over y, core).
Axes of the slice: x: 4, y: 4, z: 8, core: 2. Of those that a mesh axis runs over, the one named last changes fastest.
Arguments:
- struct_disp: float32 [3, 524288], P(None, ('group', 'span')), may hold values from -6 to 6
- interp_weight: float32 [524288, 4], P(('group', 'span')), may hold values from 0.2 to 1
- face_owner: int32 [524288, 4], P(('group', 'span')), may hold values from 0 to 31, all different within a row; in each aligned block of 2048 rows (0 to 2047, 2048 to 4095, ...) at most 512 rows name the same one
- face_row: int32 [524288, 4], P(('group', 'span')), may hold values from 0 to 20479
- skel_force: float32 [3, 16384], P(None, ('group', 'span')), may hold values from -6 to 6
- skel_coupling: float32 [6, 16384], P(None, ('group', 'span')), may hold values from 0.1 to 0.2
- skel_stiff: float32 [16384], P(('group', 'span')), may hold values from 0.05 to 0.15
- skel_edges: int32 [6, 16384], P(None, ('group', 'span')), may hold values from 0 to 16383
- block_spacing: float32 [3, 256], P(None, 'group'), may hold values from 1 to 2
Outputs:
- displacement: float32 [3, 256, 64, 6400], P(None, 'group', 'span')
- jacobian: float32 [256, 64, 6400], P('group', 'span')
Inputs may be any that keep to these rules, and one draw needn't show every extreme that they name: `face_owner`: each row names 4 different group indices; among the rows of one device no index is named more than 512 times, a bound that some block reaches.
All inputs are finite; a program needn't handle non-finite values.
Results may differ from a plain program's by a relative error of at most 0.0001.
Values sent between devices are 32-bit elements; how exact they have to be, the bound alone decides.
A program may use at most 128 MiB of HBM per device.

v0:
```python
import jax
import jax.numpy as jnp
from jax import lax
from jax.sharding import PartitionSpec as P

BPD = 8
SPAN_DEV = 8
NP = 80
ITERS = 4


def with_halo(block, sides, width):
    for axis, dim in sides:
        count = lax.axis_size(axis)
        forward = [(i, i + 1) for i in range(count - 1)]
        backward = [(target, source) for source, target in forward]
        low = lax.ppermute(
            lax.slice_in_dim(block, block.shape[dim] - width, None, axis=dim), axis, forward
        )
        high = lax.ppermute(lax.slice_in_dim(block, 0, width, axis=dim), axis, backward)
        block = jnp.concatenate([low, block, high], axis=dim)
    return block


def tfi_tables(points):
    position = jnp.arange(points * points, dtype=jnp.int32)
    first = position % points
    second = position // points
    frac_first = first.astype(jnp.float32) / (points - 1)
    frac_second = second.astype(jnp.float32) / (points - 1)
    edge_pos = jnp.arange(points, dtype=jnp.int32)[:, None]
    zero = jnp.zeros((points, points * points), jnp.float32)
    bottom = jnp.where(first[None] == edge_pos, (1.0 - frac_second)[None], zero)
    bottom = bottom.at[0].add(-(1.0 - frac_first) * (1.0 - frac_second))
    bottom = bottom.at[points - 1].add(-frac_first * (1.0 - frac_second))
    top_rows = jnp.where(first[None] == edge_pos, frac_second[None], zero)
    top_rows = top_rows.at[0].add(-(1.0 - frac_first) * frac_second)
    top_rows = top_rows.at[points - 1].add(-frac_first * frac_second)
    left_rows = jnp.where(second[None] == edge_pos, (1.0 - frac_first)[None], zero)
    right_rows = jnp.where(second[None] == edge_pos, frac_first[None], zero)
    table = jnp.concatenate([bottom, top_rows, left_rows, right_rows], axis=0)
    bubble = 16.0 * frac_first * (1.0 - frac_first) * frac_second * (1.0 - frac_second)
    return (table, bubble)


def plane_derivs(field, points):
    position = jnp.arange(points * points, dtype=jnp.int32)
    first = position % points
    second = position // points
    ahead = jnp.concatenate([field[..., 1:], field[..., -1:]], axis=-1)
    behind = jnp.concatenate([field[..., :1], field[..., :-1]], axis=-1)
    deriv_first = (
        jnp.where(first == points - 1, field, ahead) - jnp.where(first == 0, field, behind)
    ) * 0.5
    upper = jnp.concatenate([field[..., points:], field[..., -points:]], axis=-1)
    lower = jnp.concatenate([field[..., :points], field[..., :-points]], axis=-1)
    deriv_second = (
        jnp.where(second == points - 1, field, upper) - jnp.where(second == 0, field, lower)
    ) * 0.5
    return (deriv_first, deriv_second)


def metric_det(spacing, deriv_first, deriv_second, deriv_span):
    derivs = (deriv_first, deriv_second, deriv_span)
    matrix = [[derivs[col][row] for col in range(3)] for row in range(3)]
    for row in range(3):
        matrix[row][row] = matrix[row][row] + spacing[row][:, None, None]
    minor_one = matrix[1][1] * matrix[2][2] - matrix[1][2] * matrix[2][1]
    minor_two = matrix[1][0] * matrix[2][2] - matrix[1][2] * matrix[2][0]
    minor_three = matrix[1][0] * matrix[2][1] - matrix[1][1] * matrix[2][0]
    return matrix[0][0] * minor_one - matrix[0][1] * minor_two + matrix[0][2] * minor_three


def blend_layers(faces, skel_values, table, bubble):
    blended = jnp.dot(
        faces.reshape(-1, faces.shape[-1]),
        table,
        precision=lax.Precision.HIGHEST,
        preferred_element_type=jnp.float32,
    )
    shape = faces.shape[:-1] + (bubble.shape[0],)
    return blended.reshape(shape) + skel_values * bubble


def on_device(
    struct_disp,
    interp_weight,
    face_owner,
    face_row,
    skel_force,
    skel_coupling,
    skel_stiff,
    skel_edges,
    block_spacing,
):
    group_count = lax.axis_size("group")
    local_nodes = skel_force.shape[1]
    face_total = BPD * SPAN_DEV * 4 * NP
    weighted = (struct_disp[:, :, None] * interp_weight[None]).reshape(3, -1)
    owners = face_owner.reshape(-1)
    targets = face_row.reshape(-1)
    empty_faces = jnp.zeros((3, face_total), jnp.float32)
    contributions = owners.shape[0]
    capacity = 2 * contributions // group_count
    one_hot = (owners[:, None] == jnp.arange(group_count, dtype=jnp.int32)[None]).astype(jnp.int32)
    running = jnp.cumsum(one_hot, axis=0)
    slot_index = jnp.sum((running - 1) * one_hot, axis=1)
    send_values = (
        jnp.zeros((group_count, 3, capacity), jnp.float32).at[owners, :, slot_index].set(weighted.T)
    )
    send_rows = jnp.zeros((group_count, capacity), jnp.int32).at[owners, slot_index].set(targets)
    recv_values, recv_rows = (
        lax.all_to_all(send_values, "group", split_axis=0, concat_axis=0, tiled=True),
        lax.all_to_all(send_rows, "group", split_axis=0, concat_axis=0, tiled=True),
    )
    face_disp = empty_faces.at[:, recv_rows.reshape(-1)].add(
        recv_values.transpose(1, 0, 2).reshape(3, -1)
    )
    face_disp = face_disp.reshape(3, BPD, SPAN_DEV, 4 * NP)
    skeleton_rhs = skel_force + (0.25 * jnp.sum(face_disp, axis=3)).reshape(3, local_nodes)
    diagonal = skel_stiff + jnp.sum(skel_coupling, axis=0)

    def sweep(sweep_index, state):
        whole_state = lax.all_gather(state, ("group", "span"), axis=1, tiled=True)
        neighbours = whole_state[:, skel_edges]
        return (skeleton_rhs + jnp.sum(skel_coupling[None] * neighbours, axis=1)) / diagonal

    skeleton = lax.fori_loop(0, ITERS, sweep, jnp.zeros((3, local_nodes), jnp.float32))
    table, bubble = tfi_tables(NP)
    skel_layers = skeleton.reshape(3, BPD, SPAN_DEV, 1)
    displacement = blend_layers(face_disp, skel_layers, table, bubble)
    deriv_first, deriv_second = plane_derivs(displacement, NP)
    padded = with_halo(displacement, (("span", 2),), 1)
    deriv_span = (padded[:, :, 2:] - padded[:, :, :-2]) * 0.5
    jacobian = metric_det(block_spacing, deriv_first, deriv_second, deriv_span)
    return (displacement, jacobian)


def solution(mesh):
    return jax.shard_map(
        on_device,
        mesh=mesh,
        in_specs=(
            P(None, ("group", "span")),
            P(("group", "span"), None),
            P(("group", "span"), None),
            P(("group", "span"), None),
            P(None, ("group", "span")),
            P(None, ("group", "span")),
            P(("group", "span")),
            P(None, ("group", "span")),
            P(None, "group"),
        ),
        out_specs=(P(None, "group", "span", None), P("group", "span", None)),
        check_vma=False,
    )
```

profile of v0, /device:TPU:1, one launch (start us, length us, event | category | flops | bytes accessed | tf_op | source)
XLA Modules:
  0.0 607.1 jit_solution(6317149871625907783)
XLA Ops:
  0.6 1.1 copy.36
  1.8 0.6 eq.108
  2.4 0.6 eq.104
  3.1 0.7 reshape.355
  3.9 9.5 %reduce-window.6 = s32[32,64,128]{2,1,0:T(8,128)S(1)} reduce-window(s32[32,64,128]{2,1,0:T(8,128)S(1)} %fusion.34, s32[]{:T(128)} %constant.154.clone.1), window={size=1x1x128 pad=0_0x0_0x127_0}, to_apply=%region_0.0 | reduce-window | flops 33292288 | bytes 2097156 | tf_op jit(solution)/shard_map/reduce-window
  13.5 0.9 slice_reduce_fusion
  14.4 0.2 reduce-window.9
  14.6 0.3 add_add_fusion
  15.0 0.8 fusion.33
  15.8 0.1 multiply_reduce_fusion.1
  16.0 0.2 and_reduce_fusion
  16.2 0.4 copy.39
  16.6 0.6 reshape.387
  17.2 31.0 %scatter_custom_fusion.1 = s32[16384]{0:T(1024)} fusion(s32[8192]{0:T(1024)S(1)} %broadcast_select_fusion, s32[8192]{0:T(1024)S(1)} %reshape.387, s32[]{:T(128)} %constant.154.clone.1), kind=kCustom, calls=%fused_computation.84 | custom fusion | bytes 65540
  48.2 11.9 %all-to-all-start = ((s32[32,1,512]{2,1,0:T(1,128)}), s32[32,1,512]{2,1,0:T(1,128)S(1)}, u32[]{:S(2)}, u32[]{:S(2)}) async-start(s32[32,1,512]{2,1,0:T(1,128)} %bitcast.2), calls=%async_computation | async-start | bytes 131072 | tf_op jit(solution)/shard_map/all_to_all | solution.py:114
  60.3 0.3 fusion.23
  60.5 1.3 copy-done.3
  61.8 0.2 slice_add_fusion.1
  62.0 1.7 scatter-add.21
  63.7 1.1 slice_add_fusion.2
  64.8 0.8 scatter-add.30
  65.6 0.1 slice_add_fusion
  65.7 2.6 fusion.21
  68.4 0.4 copy.40
  68.8 0.4 copy.41
  69.1 0.6 mul.156
  69.8 2.4 mul.154
  72.1 28.8 %scatter_custom_fusion.2 = f32[3,16384]{0,1:T(8,128)} fusion(s32[8192]{0:T(1024)S(1)} %broadcast_select_fusion, f32[]{:T(128)} %constant.153.clone.1, f32[3,8192]{0,1:T(8,128)} %bitcast.125, f32[8192]{0:T(1024)S(1)} %mul.156), kind=kCustom, calls=%fused_computation.32 | custom fusion | flops 24576 | bytes 327684
  101.0 6.1 copy.42
  107.2 1.7 scatter-add.24
  108.9 0.6 scatter-add.31
  109.5 9.2 %all-to-all-start.1 = ((f32[32,3,512]{2,1,0:T(4,128)}), f32[32,3,512]{2,1,0:T(4,128)S(1)}, u32[]{:S(2)}, u32[]{:S(2)}) async-start(f32[32,3,512]{2,1,0:T(4,128)} %bitcast.8), calls=%async_computation.1 | async-start | bytes 524288 | tf_op jit(solution)/shard_map/all_to_all | solution.py:113
  118.8 9.6 %all-to-all-done.1 = f32[32,3,512]{2,1,0:T(4,128)S(1)} async-done(((f32[32,3,512]{2,1,0:T(4,128)}), f32[32,3,512]{2,1,0:T(4,128)S(1)}, u32[]{:S(2)}, u32[]{:S(2)}) %all-to-all-start.1) | async-done | bytes 196640 | tf_op jit(solution)/shard_map/all_to_all | solution.py:113
  128.4 5.1 copy.43
  133.5 102.3 %scatter_custom_fusion = f32[3,20480]{0,1:T(8,128)} fusion(s32[16384]{0:T(1024)S(1)} %bitcast.133, f32[16384,3]{1,0:T(8,128)} %copy.43, f32[]{:T(128)} %constant.153.clone.1), kind=kCustom, calls=%fused_computation.18 | custom fusion | flops 49152 | bytes 246272 | tf_op jit(solution)/shard_map/scatter-add | solution.py:116
  235.8 6.4 %copy.44 = f32[3,8,8,320]{3,2,1,0:T(8,128)S(1)} copy(f32[3,8,8,320]{0,3,2,1:T(8,128)} %bitcast.122) | data formatting | bytes 491520 | tf_op jit(solution)/shard_map/dot_general | solution.py:75
  242.2 5.4 reduce_sum.40
  247.6 315.2 %while.15 = (s32[]{:T(128)}, f32[3,64]{0,1:T(8,128)S(1)}, f32[6,64]{1,0:T(8,128)S(1)}, s32[6,64]{1,0:T(8,128)S(1)}, f32[3,64]{0,1:T(8,128)S(1)}, /*index=5*/f32[64]{0:T(128)S(1)}, s32[]{:T(128)}, s32[]{:T(128)}) while((s32[]{:T(128)}, f32[3,64]{0,1:T(8,128)S(1)}, f32[6,64]{1,0:T(8,128)S(1)}, s32[6,64]{1,0:T(8,128)S(1)}, ...), condition=%wide.region_10.11_spmd.clone, body=%wide.region_8.0_spmd.clone.sunk | while | flops 4867 | bytes 625759 | solution.py:128
  247.7 79.7 %all-gather.3 = f32[256,64,3]{1,2,0:T(4,128)S(1)} all-gather(f32[1,64,3]{1,2,0:T(4,128)S(1)} %select_bitcast_fusion.2), channel_id=1, replica_groups=mesh['group'=32,'span'=8] {'group','span'}, dimensions={0}, use_global_device_ids=true | all-gather | bytes 197376 | tf_op jit(solution)/shard_map/while/body/eval_jaxpr/all_gather | solution.py:124
  327.4 4.8 copy.53
  332.3 4.5 gather_fusion
  336.8 0.1 multiply_reduce_fusion.3
  337.1 65.6 %all-gather.3 = f32[256,64,3]{1,2,0:T(4,128)S(1)} all-gather(f32[1,64,3]{1,2,0:T(4,128)S(1)} %select_bitcast_fusion.2), channel_id=1, replica_groups=mesh['group'=32,'span'=8] {'group','span'}, dimensions={0}, use_global_device_ids=true | all-gather | bytes 197376 | tf_op jit(solution)/shard_map/while/body/eval_jaxpr/all_gather | solution.py:124
  402.7 4.8 copy.53
  407.6 4.5 gather_fusion
  412.1 0.1 multiply_reduce_fusion.3
  412.4 65.6 %all-gather.3 = f32[256,64,3]{1,2,0:T(4,128)S(1)} all-gather(f32[1,64,3]{1,2,0:T(4,128)S(1)} %select_bitcast_fusion.2), channel_id=1, replica_groups=mesh['group'=32,'span'=8] {'group','span'}, dimensions={0}, use_global_device_ids=true | all-gather | bytes 197376 | tf_op jit(solution)/shard_map/while/body/eval_jaxpr/all_gather | solution.py:124
  478.0 4.8 copy.53
  482.9 4.5 gather_fusion
  487.4 0.1 multiply_reduce_fusion.3
  487.7 65.6 %all-gather.3 = f32[256,64,3]{1,2,0:T(4,128)S(1)} all-gather(f32[1,64,3]{1,2,0:T(4,128)S(1)} %select_bitcast_fusion.2), channel_id=1, replica_groups=mesh['group'=32,'span'=8] {'group','span'}, dimensions={0}, use_global_device_ids=true | all-gather | bytes 197376 | tf_op jit(solution)/shard_map/while/body/eval_jaxpr/all_gather | solution.py:124
  553.3 4.8 copy.53
  558.2 4.5 gather_fusion
  562.7 0.1 multiply_reduce_fusion.3
  562.9 0.1 copy.46
  563.0 10.6 %convolution_add_fusion = f32[3,8,8,6400]{3,2,1,0:T(8,128)S(1)} fusion(f32[3,8,8,320]{3,2,1,0:T(8,128)S(1)} %copy.44, f32[80,6400]{1,0:T(8,128)} %get-tuple-element.132, f32[80,6400]{1,0:T(8,128)} %get-tuple-element.131, f32[80,6400]{1,0:T(8,128)S(1)} %scatter-add.31, f32[80,6400]{1,0:T(8,128)} %scatter-add.24, f32[6400]{0:T(1024)S(1)} %multiply_multiply_fusion, ...), kind=kOutput, calls=%fused_computation.10 | convolution fusion | flops 4727193600 | bytes 13379328 | tf_op jit(solution)/shard_map/dot_general | solution.py:75
  573.6 5.3 fusion.48
  579.0 0.7 fusion.51
  579.7 2.1 collective-permute-start
  581.8 3.8 collective-permute-start.1
  585.6 5.5 fusion.50
  591.2 1.1 collective-permute-done.1
  592.4 10.9 %fusion.12 = (f32[3,8,8,6400]{3,2,1,0:T(8,128)S(1)}, f32[3,8,8,6400]{3,2,1,0:T(8,128)S(1)}, f32[3,8,8,6400]{3,2,1,0:T(8,128)}) fusion(f32[3,8,8,6400]{3,2,1,0:T(8,128)S(1)} %convolution_add_fusion, f32[3,8,8,1]{3,2,1,0:T(8,128)S(1)} %get-tuple-element.120, f32[3,8,8,6399]{3,2,1,0:T(8,128)} %get-tuple-element.122, f32[3,8,8,6399]{3,2,1,0:T(8,128)} %get-tuple-element.121, ...), kind=kLoop, calls=%fused_computation.26 | loop fusion | flops 19660800 | bytes 40576000 | tf_op jit(solution)/shard_map/mul | solution.py:52
  603.3 3.8 fusion.25
  (73 shorter events, 1.8 us)
Async XLA Ops:
  2.4 13.4 %copy-start.12 = (s32[2]{0:T(128)S(1)}, s32[2]{0:T(128)}, u32[]{:S(2)}) copy-start(s32[2]{0:T(128)} %constant.172) | copy-start | bytes 28
  2.4 13.6 %copy-start.11 = (s32[2]{0:T(128)S(1)}, s32[2]{0:T(128)}, u32[]{:S(2)}) copy-start(s32[2]{0:T(128)} %constant.175) | copy-start | bytes 28
  2.4 13.7 %copy-start.6 = (s32[2048,4]{0,1:T(4,128)S(1)}, s32[2048,4]{0,1:T(4,128)}, u32[]{:S(2)}) copy-start(s32[2048,4]{0,1:T(4,128)} %param.22) | copy-start | bytes 98308
  14.6 51.1 %copy-start.10 = (f32[3,8]{1,0:T(4,128)S(1)}, f32[3,8]{1,0:T(4,128)}, u32[]{:S(2)}) copy-start(f32[3,8]{1,0:T(4,128)} %param.27) | copy-start | bytes 292
  16.5 51.8 %copy-start.7 = (f32[3,2048]{1,0:T(4,128)S(1)}, f32[3,2048]{1,0:T(4,128)}, u32[]{:S(2)}) copy-start(f32[3,2048]{1,0:T(4,128)} %param.19) | copy-start | bytes 73732
  48.2 61.3 %all-to-all-start = ((s32[32,1,512]{2,1,0:T(1,128)}), s32[32,1,512]{2,1,0:T(1,128)S(1)}, u32[]{:S(2)}, u32[]{:S(2)}) async-start(s32[32,1,512]{2,1,0:T(1,128)} %bitcast.2), calls=%async_computation | async-start | bytes 131072 | tf_op jit(solution)/shard_map/all_to_all | solution.py:114
  60.2 8.5 %copy-start.8 = (f32[2048,4]{0,1:T(4,128)S(1)}, f32[2048,4]{0,1:T(4,128)}, u32[]{:S(2)}) copy-start(f32[2048,4]{0,1:T(4,128)} %param.20) | copy-start | bytes 98308
  60.5 1.3 copy-start.3
  65.6 2.8 copy-start.1
  101.0 6.1 %copy-start.9 = (f32[3,64]{1,0:T(4,128)S(1)}, f32[3,64]{1,0:T(4,128)}, u32[]{:S(2)}) copy-start(f32[3,64]{1,0:T(4,128)} %param.23) | copy-start | bytes 2308
  101.0 6.2 %copy-start.4 = (f32[6,64]{1,0:T(8,128)S(1)}, f32[6,64]{1,0:T(8,128)}, u32[]{:S(2)}) copy-start(f32[6,64]{1,0:T(8,128)} %param.24) | copy-start | bytes 4612
  101.0 7.9 %copy-start.2 = (f32[80,6400]{1,0:T(8,128)S(1)}, f32[80,6400]{1,0:T(8,128)}, u32[]{:S(2)}) copy-start(f32[80,6400]{1,0:T(8,128)} %copy-done.1) | copy-start | bytes 6144004
  101.0 8.5 %copy-start.13 = (f32[64]{0:T(128)S(1)}, f32[64]{0:T(128)}, u32[]{:S(2)}) copy-start(f32[64]{0:T(128)} %param.25) | copy-start | bytes 772
  109.5 18.9 %all-to-all-start.1 = ((f32[32,3,512]{2,1,0:T(4,128)}), f32[32,3,512]{2,1,0:T(4,128)S(1)}, u32[]{:S(2)}, u32[]{:S(2)}) async-start(f32[32,3,512]{2,1,0:T(4,128)} %bitcast.8), calls=%async_computation.1 | async-start | bytes 524288 | tf_op jit(solution)/shard_map/all_to_all | solution.py:113
  242.2 5.4 copy-start.5
  573.6 18.7 %copy-start = (f32[3,8,8,6400]{3,2,1,0:T(8,128)}, f32[3,8,8,6400]{3,2,1,0:T(8,128)S(1)}, u32[]{:S(2)}) copy-start(f32[3,8,8,6400]{3,2,1,0:T(8,128)S(1)} %convolution_add_fusion) | copy-start | bytes 14745604
  579.7 11.5 %collective-permute-start = (f32[3,8,1,6400]{3,2,1,0:T(1,128)S(1)}, f32[3,8,1,6400]{3,2,1,0:T(1,128)S(1)}, u32[]{:S(2)}, u32[]{:S(2)}) collective-permute-start(f32[3,8,1,6400]{3,2,1,0:T(1,128)S(1)} %get-tuple-element.127), channel_id=1, source_target_pairs={{1,0},{2,1},{3,2},{4,3},{5,4},{6,5},{7,6},{9,8},{10,9},{11,10},{12... | collective-permute-start | bytes 1843208 | tf_op jit(solution)/shard_map/ppermute | solution.py:20
  581.8 10.6 %collective-permute-start.1 = (f32[3,8,1,6400]{3,2,1,0:T(1,128)S(1)}, f32[3,8,1,6400]{3,2,1,0:T(1,128)S(1)}, u32[]{:S(2)}, u32[]{:S(2)}) collective-permute-start(f32[3,8,1,6400]{3,2,1,0:T(1,128)S(1)} %get-tuple-element.128), channel_id=1, source_target_pairs={{0,1},{1,2},{2,3},{3,4},{4,5},{5,6},{6,7},{8,9},{9,10},{10,11},{11... | collective-permute-start | bytes 1843208 | tf_op jit(solution)/shard_map/ppermute | solution.py:17
where the time goes:
time: 608 us; the launch traced here: 607 us
  blocking collectives  276 us (45%)
  other arithmetic  168 us (28%)
  local copies, waits for them, and re-layouts  113 us (19%)
  starting transfers between devices  26.9 us (4%)
  waiting for transfers between devices  10.7 us (2%)
  matrix products  10.6 us (2%)
    all_gather x4, blocking collectives, sweep(): whole_state = lax.all_gather(state, ('group', 'span'), axis=1, tiled=True)  276 us
    scatter-add x1, other arithmetic, on_device(): empty_faces.at[:, recv_rows.reshape(-1)]  102 us
    unnamed x35, local copies, waits for them, and re-layouts  40.8 us
    unnamed x5, other arithmetic  29.2 us
    all_gather x4, local copies, waits for them, and re-layouts, sweep(): whole_state = lax.all_gather(state, ('group', 'span'), axis=1, tiled=True)  19.2 us
    gather x4, local copies, waits for them, and re-layouts, sweep(): neighbours = whole_state[:, skel_edges]  18 us
  transfers between devices with their start and end apart: 4, of which 2 were waited for; matrix products, arithmetic and copies ran while one was open for 9% of the time, Pallas kernels for 0%

commit v1 on v0

--- a/solution.py
+++ b/solution.py
@@ -121,7 +121,12 @@
     diagonal = skel_stiff + jnp.sum(skel_coupling, axis=0)
 
     def sweep(sweep_index, state):
-        whole_state = lax.all_gather(state, ("group", "span"), axis=1, tiled=True)
+        whole_state = jnp.concatenate(
+            lax.all_to_all(
+                jnp.stack([state] * lax.axis_size(("group", "span"))), ("group", "span"), 0, 0
+            ),
+            axis=1,
+        )
         neighbours = whole_state[:, skel_edges]
         return (skeleton_rhs + jnp.sum(skel_coupling[None] * neighbours, axis=1)) / diagonal
 

time: 608 us -> 442 us (0.73)
  blocking collectives: 276 us -> 0 us
  waiting for transfers between devices: 10.7 us -> 72.2 us
  starting transfers between devices: 26.9 us -> 62.7 us
  local copies, waits for them, and re-layouts: 113 us -> 121 us
    all_gather x4 -> x0, blocking collectives: 276 us -> none  [sweep(): whole_state = lax.all_gather(state, ('group', 'span'), axis=1, tiled=True)]
    all_to_all x0 -> x4, waiting for transfers between devices: none -> 61.4 us  [sweep(): lax.all_to_all(jnp.stack([state] * lax.axis_size(('group', 'span'))), ('g...]
    all_to_all x0 -> x4, starting transfers between devices: none -> 35.8 us  [sweep(): lax.all_to_all(jnp.stack([state] * lax.axis_size(('group', 'span'))), ('g...]
    reshape x0 -> x4, local copies, waits for them, and re-layouts: none -> 19.2 us  [sweep(): jnp.concatenate(lax.all_to_all(jnp.stack([state] * lax.axis_size(('group'...]
    all_gather x4 -> x0, local copies, waits for them, and re-layouts: 19.2 us -> none  [sweep(): whole_state = lax.all_gather(state, ('group', 'span'), axis=1, tiled=True)]
  transfers between devices with their start and end apart: 4 -> 8, of which waited for: 2 -> 6; matrix products, arithmetic and copies ran while one was open for 9% -> 11% of each run, Pallas kernels for 0% -> 0%
where the time goes in v1:
time: 442 us; the launch traced here: 441 us
  other arithmetic  173 us (39%)
  local copies, waits for them, and re-layouts  121 us (27%)
  waiting for transfers between devices  72.2 us (16%)
  starting transfers between devices  62.7 us (14%)
  matrix products  10.6 us (2%)
    scatter-add x1, other arithmetic, on_device(): empty_faces.at[:, recv_rows.reshape(-1)]  102 us
    all_to_all x4, waiting for transfers between devices, sweep(): lax.all_to_all(jnp.stack([state] * lax.axis_size(('group', 'span'))), ('g...  61.4 us
    unnamed x35, local copies, waits for them, and re-layouts  40.8 us
    all_to_all x4, starting transfers between devices, sweep(): lax.all_to_all(jnp.stack([state] * lax.axis_size(('group', 'span'))), ('g...  35.8 us
    unnamed x5, other arithmetic  29.2 us
    reshape x4, local copies, waits for them, and re-layouts, sweep(): jnp.concatenate(lax.all_to_all(jnp.stack([state] * lax.axis_size(('group'...  19.2 us
    gather x4, local copies, waits for them, and re-layouts, sweep(): neighbours = whole_state[:, skel_edges]  18 us
    all_to_all x1, starting transfers between devices, on_device(): lax.all_to_all(send_rows, 'group', split_axis=0, concat_axis=0, tiled=True)  12 us
  transfers between devices with their start and end apart: 8, of which 6 were waited for; matrix products, arithmetic and copies ran while one was open for 11% of the time, Pallas kernels for 0%

profile of v1, /device:TPU:1, one launch (start us, length us, event | category | flops | bytes accessed | tf_op | source)
XLA Modules:
  0.0 440.6 jit_solution(14900425258373399245)
XLA Ops:
  0.6 1.1 copy.36
  1.8 0.6 eq.108
  2.4 0.6 eq.104
  3.1 0.7 reshape.363
  4.1 9.5 %reduce-window.6 = s32[32,64,128]{2,1,0:T(8,128)S(1)} reduce-window(s32[32,64,128]{2,1,0:T(8,128)S(1)} %fusion.34, s32[]{:T(128)} %constant.154.clone.1), window={size=1x1x128 pad=0_0x0_0x127_0}, to_apply=%region_0.0 | reduce-window | flops 33292288 | bytes 2097156 | tf_op jit(solution)/shard_map/reduce-window
  13.6 0.9 slice_reduce_fusion
  15.1 0.8 fusion.33
  16.7 0.6 reshape.395
  17.6 1.3 copy-done.3
  19.1 1.7 scatter-add.21
  20.8 1.1 slice_add_fusion.2
  21.9 0.6 scatter-add.30
  22.7 31.0 %scatter_custom_fusion.1 = s32[16384]{0:T(1024)} fusion(s32[8192]{0:T(1024)S(1)} %broadcast_select_fusion.1, s32[8192]{0:T(1024)S(1)} %reshape.395, s32[]{:T(128)} %constant.154.clone.1), kind=kCustom, calls=%fused_computation.84 | custom fusion | bytes 65540
  53.7 2.3 fusion.21
  56.0 12.0 %all-to-all-start.1 = ((s32[32,1,512]{2,1,0:T(1,128)}), s32[32,1,512]{2,1,0:T(1,128)S(1)}, u32[]{:S(2)}, u32[]{:S(2)}) async-start(s32[32,1,512]{2,1,0:T(1,128)} %bitcast.2), calls=%async_computation.1 | async-start | bytes 131072 | tf_op jit(solution)/shard_map/all_to_all | solution.py:114
  68.8 0.6 mul.156
  69.5 2.4 mul.154
  71.9 28.8 %scatter_custom_fusion.2 = f32[3,16384]{0,1:T(8,128)} fusion(s32[8192]{0:T(1024)S(1)} %broadcast_select_fusion.1, f32[]{:T(128)} %constant.153.clone.1, f32[3,8192]{0,1:T(8,128)} %bitcast.121, f32[8192]{0:T(1024)S(1)} %mul.156), kind=kCustom, calls=%fused_computation.32 | custom fusion | flops 24576 | bytes 327684
  100.7 6.1 %copy.42 = f32[3,32,512]{2,0,1:T(4,128)} copy(f32[3,32,512]{0,2,1:T(8,128)} %bitcast.120) | data formatting | bytes 393216
  106.9 1.7 scatter-add.24
  108.6 0.6 scatter-add.31
  109.2 9.1 %all-to-all-start.2 = ((f32[32,3,512]{2,1,0:T(4,128)}), f32[32,3,512]{2,1,0:T(4,128)S(1)}, u32[]{:S(2)}, u32[]{:S(2)}) async-start(f32[32,3,512]{2,1,0:T(4,128)} %bitcast.8), calls=%async_computation.2 | async-start | bytes 524288 | tf_op jit(solution)/shard_map/all_to_all | solution.py:113
  118.4 9.6 %all-to-all-done.2 = f32[32,3,512]{2,1,0:T(4,128)S(1)} async-done(((f32[32,3,512]{2,1,0:T(4,128)}), f32[32,3,512]{2,1,0:T(4,128)S(1)}, u32[]{:S(2)}, u32[]{:S(2)}) %all-to-all-start.2) | async-done | bytes 196640 | tf_op jit(solution)/shard_map/all_to_all | solution.py:113
  128.0 5.1 %copy.43 = f32[16384,3]{1,0:T(8,128)} copy(f32[16384,3]{0,1:T(4,128)S(1)} %bitcast.125) | data formatting | bytes 393216 | tf_op jit(solution)/shard_map/reshape | solution.py:117
  133.0 102.3 %scatter_custom_fusion = f32[3,20480]{0,1:T(8,128)} fusion(s32[16384]{0:T(1024)S(1)} %bitcast.129, f32[16384,3]{1,0:T(8,128)} %copy.43, f32[]{:T(128)} %constant.153.clone.1), kind=kCustom, calls=%fused_computation.18 | custom fusion | flops 49152 | bytes 246272 | tf_op jit(solution)/shard_map/scatter-add | solution.py:116
  235.3 6.4 %copy.44 = f32[3,8,8,320]{3,2,1,0:T(8,128)S(1)} copy(f32[3,8,8,320]{0,3,2,1:T(8,128)} %bitcast.117) | data formatting | bytes 491520 | tf_op jit(solution)/shard_map/dot_general | solution.py:75
  241.8 5.4 %reduce_sum.40 = f32[3,8,8]{0,2,1:T(8,128)S(1)} reduce(f32[3,8,8,320]{0,3,2,1:T(8,128)} %bitcast.118, f32[]{:T(128)} %constant.153.clone.1), dimensions={3}, to_apply=%region_6.7 | reduce | flops 61248 | bytes 246532 | tf_op jit(solution)/shard_map/reduce_sum | solution.py:120
  247.2 149.2 %while.15 = (s32[]{:T(128)}, f32[3,64]{0,1:T(8,128)S(1)}, f32[6,64]{1,0:T(8,128)S(1)}, s32[6,64]{1,0:T(8,128)S(1)}, f32[3,64]{0,1:T(8,128)S(1)}, /*index=5*/f32[64]{0:T(128)S(1)}, s32[]{:T(128)}, s32[]{:T(128)}, f32[]{:T(128)}) while((s32[]{:T(128)}, f32[3,64]{0,1:T(8,128)S(1)}, f32[6,64]{1,0:T(8,128)S(1)}, ...), condition=%wide.region_10.11_spmd.clone, body=%wide.region_8.0_spmd.clone.sunk | while | flops 4867 | bytes 2526355 | solution.py:133
  247.4 1.2 reshape.430
  248.5 20.3 %all-to-all-start = ((f32[256,1,192]{2,1,0:T(1,128)}), f32[256,1,192]{2,1,0:T(1,128)S(1)}, u32[]{:S(2)}, u32[]{:S(2)}) async-start(f32[256,1,192]{2,1,0:T(1,128)} %reshape.430), calls=%async_computation | async-start | bytes 524288 | tf_op jit(solution)/shard_map/while/body/eval_jaxpr/all_to_all | solution.py:125
  269.0 15.4 %all-to-all-done = f32[256,1,192]{2,1,0:T(1,128)S(1)} async-done(((f32[256,1,192]{2,1,0:T(1,128)}), f32[256,1,192]{2,1,0:T(1,128)S(1)}, u32[]{:S(2)}, u32[]{:S(2)}) %all-to-all-start) | async-done | bytes 196640 | tf_op jit(solution)/shard_map/while/body/eval_jaxpr/all_to_all | solution.py:125
  284.4 0.5 broadcast.630
  284.9 1.3 reduce.23
  286.4 4.8 %copy.53 = f32[3,256,64]{0,2,1:T(8,128)} copy(f32[3,256,64]{2,0,1:T(4,128)S(1)} %bitcast.119) | data formatting | bytes 393216 | tf_op jit(solution)/shard_map/while/body/eval_jaxpr/reshape | solution.py:124
  291.2 4.5 %gather_fusion = f32[384,3]{1,0:T(8,128)S(1)} fusion(f32[3,16384]{0,1:T(8,128)} %bitcast.116, s32[1024]{0:T(1024)S(1)} %pad_clamp_fusion.2), kind=kCustom, calls=%fused_computation.clone.clone.1 | custom fusion | bytes 10752 | tf_op jit(solution)/shard_map/while/body/eval_jaxpr/gather | solution.py:130
  296.1 1.2 reshape.430
  297.3 5.2 %all-to-all-start = ((f32[256,1,192]{2,1,0:T(1,128)}), f32[256,1,192]{2,1,0:T(1,128)S(1)}, u32[]{:S(2)}, u32[]{:S(2)}) async-start(f32[256,1,192]{2,1,0:T(1,128)} %reshape.430), calls=%async_computation | async-start | bytes 524288 | tf_op jit(solution)/shard_map/while/body/eval_jaxpr/all_to_all | solution.py:125
  302.5 15.3 %all-to-all-done = f32[256,1,192]{2,1,0:T(1,128)S(1)} async-done(((f32[256,1,192]{2,1,0:T(1,128)}), f32[256,1,192]{2,1,0:T(1,128)S(1)}, u32[]{:S(2)}, u32[]{:S(2)}) %all-to-all-start) | async-done | bytes 196640 | tf_op jit(solution)/shard_map/while/body/eval_jaxpr/all_to_all | solution.py:125
  317.9 0.5 broadcast.630
  318.4 1.3 reduce.23
  319.9 4.8 %copy.53 = f32[3,256,64]{0,2,1:T(8,128)} copy(f32[3,256,64]{2,0,1:T(4,128)S(1)} %bitcast.119) | data formatting | bytes 393216 | tf_op jit(solution)/shard_map/while/body/eval_jaxpr/reshape | solution.py:124
  324.7 4.5 %gather_fusion = f32[384,3]{1,0:T(8,128)S(1)} fusion(f32[3,16384]{0,1:T(8,128)} %bitcast.116, s32[1024]{0:T(1024)S(1)} %pad_clamp_fusion.2), kind=kCustom, calls=%fused_computation.clone.clone.1 | custom fusion | bytes 10752 | tf_op jit(solution)/shard_map/while/body/eval_jaxpr/gather | solution.py:130
  329.6 1.2 reshape.430
  330.8 5.2 %all-to-all-start = ((f32[256,1,192]{2,1,0:T(1,128)}), f32[256,1,192]{2,1,0:T(1,128)S(1)}, u32[]{:S(2)}, u32[]{:S(2)}) async-start(f32[256,1,192]{2,1,0:T(1,128)} %reshape.430), calls=%async_computation | async-start | bytes 524288 | tf_op jit(solution)/shard_map/while/body/eval_jaxpr/all_to_all | solution.py:125
  336.0 15.3 %all-to-all-done = f32[256,1,192]{2,1,0:T(1,128)S(1)} async-done(((f32[256,1,192]{2,1,0:T(1,128)}), f32[256,1,192]{2,1,0:T(1,128)S(1)}, u32[]{:S(2)}, u32[]{:S(2)}) %all-to-all-start) | async-done | bytes 196640 | tf_op jit(solution)/shard_map/while/body/eval_jaxpr/all_to_all | solution.py:125
  351.9 1.3 reduce.23
  353.4 4.8 %copy.53 = f32[3,256,64]{0,2,1:T(8,128)} copy(f32[3,256,64]{2,0,1:T(4,128)S(1)} %bitcast.119) | data formatting | bytes 393216 | tf_op jit(solution)/shard_map/while/body/eval_jaxpr/reshape | solution.py:124
  358.2 4.5 %gather_fusion = f32[384,3]{1,0:T(8,128)S(1)} fusion(f32[3,16384]{0,1:T(8,128)} %bitcast.116, s32[1024]{0:T(1024)S(1)} %pad_clamp_fusion.2), kind=kCustom, calls=%fused_computation.clone.clone.1 | custom fusion | bytes 10752 | tf_op jit(solution)/shard_map/while/body/eval_jaxpr/gather | solution.py:130
  363.1 1.2 reshape.430
  364.3 5.2 %all-to-all-start = ((f32[256,1,192]{2,1,0:T(1,128)}), f32[256,1,192]{2,1,0:T(1,128)S(1)}, u32[]{:S(2)}, u32[]{:S(2)}) async-start(f32[256,1,192]{2,1,0:T(1,128)} %reshape.430), calls=%async_computation | async-start | bytes 524288 | tf_op jit(solution)/shard_map/while/body/eval_jaxpr/all_to_all | solution.py:125
  369.5 15.3 %all-to-all-done = f32[256,1,192]{2,1,0:T(1,128)S(1)} async-done(((f32[256,1,192]{2,1,0:T(1,128)}), f32[256,1,192]{2,1,0:T(1,128)S(1)}, u32[]{:S(2)}, u32[]{:S(2)}) %all-to-all-start) | async-done | bytes 196640 | tf_op jit(solution)/shard_map/while/body/eval_jaxpr/all_to_all | solution.py:125
  384.9 0.5 broadcast.630
  385.4 1.3 reduce.23
  386.9 4.8 %copy.53 = f32[3,256,64]{0,2,1:T(8,128)} copy(f32[3,256,64]{2,0,1:T(4,128)S(1)} %bitcast.119) | data formatting | bytes 393216 | tf_op jit(solution)/shard_map/while/body/eval_jaxpr/reshape | solution.py:124
  391.7 4.5 %gather_fusion = f32[384,3]{1,0:T(8,128)S(1)} fusion(f32[3,16384]{0,1:T(8,128)} %bitcast.116, s32[1024]{0:T(1024)S(1)} %pad_clamp_fusion.2), kind=kCustom, calls=%fused_computation.clone.clone.1 | custom fusion | bytes 10752 | tf_op jit(solution)/shard_map/while/body/eval_jaxpr/gather | solution.py:130
  396.5 10.6 %convolution_add_fusion = f32[3,8,8,6400]{3,2,1,0:T(8,128)S(1)} fusion(f32[3,8,8,320]{3,2,1,0:T(8,128)S(1)} %copy.44, f32[80,6400]{1,0:T(8,128)} %get-tuple-element.132, f32[80,6400]{1,0:T(8,128)} %get-tuple-element.131, f32[80,6400]{1,0:T(8,128)S(1)} %scatter-add.31, f32[80,6400]{1,0:T(8,128)} %scatter-add.24, f32[6400]{0:T(1024)S(1)} %multiply_multiply_fusion, ...), kind=kOutput, calls=%fused_computation.10 | convolution fusion | flops 4727193600 | bytes 13379328 | tf_op jit(solution)/shard_map/dot_general | solution.py:75
  407.2 5.3 %fusion.48 = (f32[3,8,8,6399]{3,2,1,0:T(8,128)}, f32[3,8,8,6399]{3,2,1,0:T(8,128)}) fusion(f32[3,8,8,6400]{3,2,1,0:T(8,128)S(1)} %convolution_add_fusion), kind=kLoop, calls=%fused_computation.116 | loop fusion | bytes 19657728 | tf_op jit(solution)/shard_map/slice | solution.py:51
  412.5 0.7 fusion.51
  413.2 1.9 collective-permute-start
  415.1 3.9 collective-permute-start.1
  419.0 5.5 %fusion.50 = (f32[3,8,8,6320]{3,2,1,0:T(8,128)}, f32[3,8,8,6320]{3,2,1,0:T(8,128)}) fusion(f32[3,8,8,6400]{3,2,1,0:T(8,128)S(1)} %convolution_add_fusion), kind=kLoop, calls=%fused_computation.118 | loop fusion | bytes 19415040 | tf_op jit(solution)/shard_map/slice | solution.py:56
  424.7 1.2 collective-permute-done.1
  425.8 10.9 %fusion.12 = (f32[3,8,8,6400]{3,2,1,0:T(8,128)S(1)}, f32[3,8,8,6400]{3,2,1,0:T(8,128)S(1)}, f32[3,8,8,6400]{3,2,1,0:T(8,128)}) fusion(f32[3,8,8,6400]{3,2,1,0:T(8,128)S(1)} %convolution_add_fusion, f32[3,8,8,1]{3,2,1,0:T(8,128)S(1)} %get-tuple-element.120, f32[3,8,8,6399]{3,2,1,0:T(8,128)} %get-tuple-element.122, f32[3,8,8,6399]{3,2,1,0:T(8,128)} %get-tuple-element.121, ...), kind=kLoop, calls=%fused_computation.26 | loop fusion | flops 19660800 | bytes 40576000 | tf_op jit(solution)/shard_map/mul | solution.py:52
  436.8 3.8 fusion.25
  (97 shorter events, 6.5 us)
Async XLA Ops:
  2.4 13.6 %copy-start.12 = (s32[2]{0:T(128)S(1)}, s32[2]{0:T(128)}, u32[]{:S(2)}) copy-start(s32[2]{0:T(128)} %constant.172) | copy-start | bytes 28
  2.4 13.7 %copy-start.11 = (s32[2]{0:T(128)S(1)}, s32[2]{0:T(128)}, u32[]{:S(2)}) copy-start(s32[2]{0:T(128)} %constant.175) | copy-start | bytes 28
  2.4 13.9 %copy-start.6 = (s32[2048,4]{0,1:T(4,128)S(1)}, s32[2048,4]{0,1:T(4,128)}, u32[]{:S(2)}) copy-start(s32[2048,4]{0,1:T(4,128)} %param.22) | copy-start | bytes 98308
  14.7 7.9 %copy-start.10 = (f32[3,8]{1,0:T(4,128)S(1)}, f32[3,8]{1,0:T(4,128)}, u32[]{:S(2)}) copy-start(f32[3,8]{1,0:T(4,128)} %param.27) | copy-start | bytes 292
  16.7 51.4 %copy-start.7 = (f32[3,2048]{1,0:T(4,128)S(1)}, f32[3,2048]{1,0:T(4,128)}, u32[]{:S(2)}) copy-start(f32[3,2048]{1,0:T(4,128)} %param.19) | copy-start | bytes 73732
  17.3 51.1 %copy-start.8 = (f32[2048,4]{0,1:T(4,128)S(1)}, f32[2048,4]{0,1:T(4,128)}, u32[]{:S(2)}) copy-start(f32[2048,4]{0,1:T(4,128)} %param.20) | copy-start | bytes 98308
  17.6 1.3 copy-start.3
  22.5 45.6 %copy-start.1 = (f32[80,6400]{1,0:T(8,128)}, f32[80,6400]{1,0:T(8,128)S(1)}, u32[]{:S(2)}) copy-start(f32[80,6400]{1,0:T(8,128)S(1)} %scatter-add.30) | copy-start | bytes 6144004
  56.0 53.3 %all-to-all-start.1 = ((s32[32,1,512]{2,1,0:T(1,128)}), s32[32,1,512]{2,1,0:T(1,128)S(1)}, u32[]{:S(2)}, u32[]{:S(2)}) async-start(s32[32,1,512]{2,1,0:T(1,128)} %bitcast.2), calls=%async_computation.1 | async-start | bytes 131072 | tf_op jit(solution)/shard_map/all_to_all | solution.py:114
  100.7 6.1 %copy-start.9 = (f32[3,64]{1,0:T(4,128)S(1)}, f32[3,64]{1,0:T(4,128)}, u32[]{:S(2)}) copy-start(f32[3,64]{1,0:T(4,128)} %param.23) | copy-start | bytes 2308
  100.7 6.2 %copy-start.4 = (f32[6,64]{1,0:T(8,128)S(1)}, f32[6,64]{1,0:T(8,128)}, u32[]{:S(2)}) copy-start(f32[6,64]{1,0:T(8,128)} %param.24) | copy-start | bytes 4612
  100.7 7.9 %copy-start.2 = (f32[80,6400]{1,0:T(8,128)S(1)}, f32[80,6400]{1,0:T(8,128)}, u32[]{:S(2)}) copy-start(f32[80,6400]{1,0:T(8,128)} %copy-done.1) | copy-start | bytes 6144004
  100.7 8.5 %copy-start.13 = (f32[64]{0:T(128)S(1)}, f32[64]{0:T(128)}, u32[]{:S(2)}) copy-start(f32[64]{0:T(128)} %param.25) | copy-start | bytes 772
  109.2 18.7 %all-to-all-start.2 = ((f32[32,3,512]{2,1,0:T(4,128)}), f32[32,3,512]{2,1,0:T(4,128)S(1)}, u32[]{:S(2)}, u32[]{:S(2)}) async-start(f32[32,3,512]{2,1,0:T(4,128)} %bitcast.8), calls=%async_computation.2 | async-start | bytes 524288 | tf_op jit(solution)/shard_map/all_to_all | solution.py:113
  241.7 5.4 %copy-start.5 = (s32[6,64]{1,0:T(8,128)S(1)}, s32[6,64]{1,0:T(8,128)}, u32[]{:S(2)}) copy-start(s32[6,64]{1,0:T(8,128)} %param.26) | copy-start | bytes 4612
  248.5 35.8 %all-to-all-start = ((f32[256,1,192]{2,1,0:T(1,128)}), f32[256,1,192]{2,1,0:T(1,128)S(1)}, u32[]{:S(2)}, u32[]{:S(2)}) async-start(f32[256,1,192]{2,1,0:T(1,128)} %reshape.430), calls=%async_computation | async-start | bytes 524288 | tf_op jit(solution)/shard_map/while/body/eval_jaxpr/all_to_all | solution.py:125
  297.3 20.6 %all-to-all-start = ((f32[256,1,192]{2,1,0:T(1,128)}), f32[256,1,192]{2,1,0:T(1,128)S(1)}, u32[]{:S(2)}, u32[]{:S(2)}) async-start(f32[256,1,192]{2,1,0:T(1,128)} %reshape.430), calls=%async_computation | async-start | bytes 524288 | tf_op jit(solution)/shard_map/while/body/eval_jaxpr/all_to_all | solution.py:125
  330.8 20.6 %all-to-all-start = ((f32[256,1,192]{2,1,0:T(1,128)}), f32[256,1,192]{2,1,0:T(1,128)S(1)}, u32[]{:S(2)}, u32[]{:S(2)}) async-start(f32[256,1,192]{2,1,0:T(1,128)} %reshape.430), calls=%async_computation | async-start | bytes 524288 | tf_op jit(solution)/shard_map/while/body/eval_jaxpr/all_to_all | solution.py:125
  364.3 20.6 %all-to-all-start = ((f32[256,1,192]{2,1,0:T(1,128)}), f32[256,1,192]{2,1,0:T(1,128)S(1)}, u32[]{:S(2)}, u32[]{:S(2)}) async-start(f32[256,1,192]{2,1,0:T(1,128)} %reshape.430), calls=%async_computation | async-start | bytes 524288 | tf_op jit(solution)/shard_map/while/body/eval_jaxpr/all_to_all | solution.py:125
  407.1 18.7 %copy-start = (f32[3,8,8,6400]{3,2,1,0:T(8,128)}, f32[3,8,8,6400]{3,2,1,0:T(8,128)S(1)}, u32[]{:S(2)}) copy-start(f32[3,8,8,6400]{3,2,1,0:T(8,128)S(1)} %convolution_add_fusion) | copy-start | bytes 14745604
  413.2 11.5 %collective-permute-start = (f32[3,8,1,6400]{3,2,1,0:T(1,128)S(1)}, f32[3,8,1,6400]{3,2,1,0:T(1,128)S(1)}, u32[]{:S(2)}, u32[]{:S(2)}) collective-permute-start(f32[3,8,1,6400]{3,2,1,0:T(1,128)S(1)} %get-tuple-element.127), channel_id=1, source_target_pairs={{1,0},{2,1},{3,2},{4,3},{5,4},{6,5},{7,6},{9,8},{10,9},{11,10},{12... | collective-permute-start | bytes 1843208 | tf_op jit(solution)/shard_map/ppermute | solution.py:20
  415.1 10.7 %collective-permute-start.1 = (f32[3,8,1,6400]{3,2,1,0:T(1,128)S(1)}, f32[3,8,1,6400]{3,2,1,0:T(1,128)S(1)}, u32[]{:S(2)}, u32[]{:S(2)}) collective-permute-start(f32[3,8,1,6400]{3,2,1,0:T(1,128)S(1)} %get-tuple-element.128), channel_id=1, source_target_pairs={{0,1},{1,2},{2,3},{3,4},{4,5},{5,6},{6,7},{8,9},{9,10},{10,11},{11... | collective-permute-start | bytes 1843208 | tf_op jit(solution)/shard_map/ppermute | solution.py:17
